TPU v7x, 32 devices: a whole 2x2x4 slice. The times are simulated.
32 devices in a mesh: groups: 2 (over y), tok: 4 (over z), mod: 2 (over x), fsdp: 2 (over core).
Axes of the slice: x: 2, y: 2, z: 4, core: 2. Of those that a mesh axis runs over, the one named last changes fastest.
Arguments:
- residual: bfloat16 [1024, 4096], P(('groups', 'tok'), ('fsdp', 'mod')), parts along dimension 0, may hold values from -30 to 30
- context: bfloat16 [1024, 4096], P(('groups', 'tok'), ('mod', 'fsdp')), parts along dimension 0, may hold values from -6 to 6
- out_proj: bfloat16 [4096, 4096], P('tok', ('fsdp', 'mod')), may hold values from -0.09375 to 0.09375
- norm_gain: bfloat16 [2, 4096], P(None, ('fsdp', 'mod')), may hold values from 0.099609375 to 1.8984375
- router_weight: bfloat16 [4096, 4], P(('fsdp', 'mod')), may hold values from -0.25 to 0.25
- block_modality: int32 [8], P(('groups', 'tok')), parts along dimension 0, may hold values from 0 to 1, as said below
- expert_rows: int32 [4, 128], P(None, ('groups', 'tok')), parts along dimension 1, may hold values from -1 to 127, as said below
- gate_weight: bfloat16 [4, 4096, 11008], P('mod', 'fsdp', 'tok'), may hold values from -0.09375 to 0.09375
- up_weight: bfloat16 [4, 4096, 11008], P('mod', 'fsdp', 'tok'), may hold values from -0.09375 to 0.09375
- down_weight: bfloat16 [4, 11008, 4096], P('mod', 'tok', 'fsdp'), may hold values from -0.0546875 to 0.0546875
Outputs:
- expert_out: bfloat16 [1024, 4096], P(('groups', 'tok'), ('fsdp', 'mod')), parts along dimension 0
There are 2 independent parts, one for each index of `groups`. A program takes and returns all parts, laid end to end along the dimension named above; an argument that names none is the same for every part. Nothing has to cross between parts.
Inputs may be any that keep to these rules, and one draw needn't show every extreme that they name: `block_modality`: both modalities occur in every window. `expert_rows`: slot s = t * 16 + j of expert e names a row among tokens t * 128 to (t + 1) * 128 - 1, or is -1 if unused. Experts below 2 take only text tokens, the others only image tokens; no expert takes a token twice; in each aligned block of 16 slots the used ones come first; every expert fills all 16 slots of at least one index of tok whose tokens have the expert's modality.
All inputs are finite; a program needn't handle non-finite values.
Results may differ from a plain program's by a relative error of at most 0.02.
Values may be sent and summed in bfloat16 or wider, within the bound.
No kernel may reach another device: no remote copies, remote signals or barrier semaphores. Data moves between devices by JAX's collectives and lax.ppermute only.
A program may use at most 192 MiB of HBM per device.

v0:
```python
import jax
import jax.numpy as jnp
from jax import lax
from jax.sharding import PartitionSpec as P

D = 4096
BLOCK = 128


def local(
    residual,
    context,
    out_proj,
    norm_gain,
    router_weight,
    block_modality,
    expert_rows,
    gate_weight,
    up_weight,
    down_weight,
):
    full_context = lax.all_gather(context, ("mod", "fsdp"), axis=1, tiled=True)
    token_count = residual.shape[0]
    projected = jnp.dot(
        full_context,
        lax.all_gather(out_proj, "tok", axis=0, tiled=True),
        preferred_element_type=jnp.float32,
    )
    hidden = residual.astype(jnp.float32) + projected
    token_mod = jnp.repeat(block_modality, BLOCK)
    gain_table = norm_gain.astype(jnp.float32)
    token_gain = jnp.where(token_mod[:, None] == 0, gain_table[0][None, :], gain_table[1][None, :])
    gained = hidden * token_gain
    router_table = router_weight.astype(jnp.float32)
    squares = jnp.sum(hidden * hidden, axis=1)
    square_total = lax.psum(squares, ("mod", "fsdp"))
    inverse = lax.rsqrt(square_total / D + 1e-05)
    normed = gained * inverse[:, None]
    logits = lax.psum(
        jnp.dot(normed, router_table, precision=lax.Precision.HIGHEST), ("mod", "fsdp")
    )
    score = jax.nn.sigmoid(logits)
    normed_rows = normed.astype(jnp.bfloat16)
    local_experts = gate_weight.shape[0]
    first_expert = lax.axis_index("mod") * local_experts
    row_ids = lax.iota(jnp.int32, token_count)
    own_rows = lax.dynamic_slice_in_dim(expert_rows, first_expert, local_experts, 0)
    own_pick = (own_rows[:, :, None] == row_ids[None, None, :]).astype(jnp.bfloat16)
    half_rows = lax.all_gather(normed_rows, "mod", axis=1, tiled=True)
    chosen = jnp.einsum(
        "ecr,rd->ecd", own_pick, half_rows, preferred_element_type=jnp.float32
    ).astype(jnp.bfloat16)
    unit_count = gate_weight.shape[2]
    piece = lax.all_gather(chosen, "tok", axis=1, tiled=True)
    gate_part = jnp.einsum("esd,edf->esf", piece, gate_weight, preferred_element_type=jnp.float32)
    up_part = jnp.einsum("esd,edf->esf", piece, up_weight, preferred_element_type=jnp.float32)
    partial_in = jnp.concatenate((gate_part, up_part), axis=2)
    summed_in = lax.psum(partial_in.astype(jnp.bfloat16), "fsdp").astype(jnp.float32)
    activation = (jax.nn.silu(summed_in[:, :, :unit_count]) * summed_in[:, :, unit_count:]).astype(
        jnp.bfloat16
    )
    expert_value = lax.psum_scatter(
        jnp.einsum(
            "esf,efd->sed", activation, down_weight, preferred_element_type=jnp.float32
        ).astype(jnp.bfloat16),
        "tok",
        scatter_dimension=0,
        tiled=True,
    ).astype(jnp.float32)
    own_score = lax.dynamic_slice_in_dim(score, first_expert, local_experts, 1)
    pick_table = own_pick.astype(jnp.float32)
    slot_score = jnp.einsum("ecr,re->ce", pick_table, own_score, precision=lax.Precision.HIGHEST)
    scaled = expert_value * slot_score[:, :, None]
    mixed_rows = jnp.einsum("ecr,ced->rd", pick_table, scaled, precision=lax.Precision.HIGHEST)
    combined = lax.psum_scatter(
        mixed_rows.astype(jnp.bfloat16), "mod", scatter_dimension=1, tiled=True
    )
    return combined


def solution(mesh):
    placed = (
        P(("groups", "tok"), ("fsdp", "mod")),
        P(("groups", "tok"), ("mod", "fsdp")),
        P("tok", ("fsdp", "mod")),
        P(None, ("fsdp", "mod")),
        P(("fsdp", "mod"), None),
        P(("groups", "tok")),
        P(None, ("groups", "tok")),
        P("mod", "fsdp", "tok"),
        P("mod", "fsdp", "tok"),
        P("mod", "tok", "fsdp"),
    )
    return jax.shard_map(
        local,
        mesh=mesh,
        in_specs=placed,
        out_specs=P(("groups", "tok"), ("fsdp", "mod")),
        check_vma=False,
    )
```

profile of v0, /device:TPU:0, one launch (start us, length us, event | category | flops | bytes accessed | tf_op | source)
XLA Modules:
  0.0 316.3 jit_solution(1377281258367514044)
XLA Ops:
  6.5 0.7 all-gather.3.cloned.1.call-update
  7.3 0.7 all-gather.5.cloned.1.call-update
  8.7 0.7 convert_element_type.35
  9.4 0.7 constant_dynamic-slice_fusion.1
  10.1 18.3 %all-gather.3.cloned.1.call-done = bf16[128,4096]{1,0:T(8,128)(2,1)} async-done(((bf16[128,1024]{1,0:T(8,128)(2,1)}), bf16[128,4096]{1,0:T(8,128)(2,1)}) %all-gather.3.cloned.1.call-update) | async-done | bytes 1048592 | tf_op jit(solution)/shard_map/all_gather | solution.py:22
  28.4 151.2 %all-gather.5.cloned.1.call-done = bf16[4096,1024]{1,0:T(8,128)(2,1)} async-done(((bf16[1024,1024]{1,0:T(8,128)(2,1)}), bf16[4096,1024]{1,0:T(8,128)(2,1)}) %all-gather.5.cloned.1.call-update) | async-done | bytes 8388624 | tf_op jit(solution)/shard_map/all_gather | solution.py:26
  179.6 5.0 %multiply_reduce_fusion = (f32[128]{0:T(128)S(1)}, f32[128,1024]{1,0:T(8,128)S(1)}) fusion(bf16[128,4096]{1,0:T(8,128)(2,1)} %all-gather.3.cloned.1.call-done, bf16[4096,1024]{1,0:T(8,128)(2,1)} %all-gather.5.cloned.1.call-done, bf16[128,1024]{1,0:T(8,128)(2,1)} %param.10), kind=kOutput, calls=%fused_computation.13 | convolution fusion | flops 1074265984 | bytes 10224128 | tf_op jit(solution)/shard_map/dot_general | solution.py:24
  184.6 6.8 %psum.21 = f32[128]{0:T(128)S(1)} all-reduce(f32[128]{0:T(128)S(1)} %get-tuple-element.5), channel_id=1, replica_groups=mesh['groups'=2,'tok'=4,'mod'=2,'fsdp'=2] {'mod','fsdp'}, use_global_device_ids=true, to_apply=%region_1.2 | all-reduce | flops 128 | bytes 1024 | tf_op jit(solution)/shard_map/psum | solution.py:36
  191.5 0.1 fusion.7
  191.6 7.6 %all_gather.14 = bf16[128,2048]{1,0:T(8,128)(2,1)S(1)} all-gather(bf16[128,1024]{1,0:T(8,128)(2,1)S(1)} %fusion.7), channel_id=1, replica_groups=mesh['groups'=2,'tok'=4,'mod'=2,'fsdp'=2] {'mod'}, dimensions={1}, use_global_device_ids=true | all-gather | bytes 786432 | tf_op jit(solution)/shard_map/all_gather | solution.py:49
  199.1 0.2 convolution_convert_fusion.3
  199.4 14.7 %all_gather.15 = bf16[2,64,2048]{2,1,0:T(8,128)(2,1)S(1)} all-gather(bf16[2,16,2048]{2,1,0:T(8,128)(2,1)S(1)} %convolution_convert_fusion.3), channel_id=1, replica_groups=mesh['groups'=2,'tok'=4,'mod'=2,'fsdp'=2] {'tok'}, dimensions={1}, use_global_device_ids=true | all-gather | bytes 655360 | tf_op jit(solution)/shard_map/all_gather | solution.py:54
  214.1 11.3 %convolution_convert_fusion = bf16[2,64,2752]{2,1,0:T(8,128)(2,1)S(1)} fusion(bf16[2,64,2048]{2,1,0:T(8,128)(2,1)S(1)} %all_gather.15, bf16[2,2048,2752]{1,2,0:T(8,128)(2,1)} %param.18), kind=kOutput, calls=%fused_computation | convolution fusion | flops 1443192832 | bytes 23773184 | tf_op jit(solution)/shard_map/esd,edf->esf/dot_general | solution.py:56
  225.4 11.3 %convolution_convert_fusion.1 = bf16[2,64,2752]{2,1,0:T(8,128)(2,1)S(1)} fusion(bf16[2,64,2048]{2,1,0:T(8,128)(2,1)S(1)} %all_gather.15, bf16[2,2048,2752]{1,2,0:T(8,128)(2,1)} %param.17), kind=kOutput, calls=%fused_computation.1 | convolution fusion | flops 1443192832 | bytes 23773184 | tf_op jit(solution)/shard_map/esd,edf->esf/dot_general | solution.py:55
  236.7 1.4 pad_maximum_fusion
  238.2 19.4 %all-reduce.2.cloned.1.call-done = bf16[2,64,5504]{2,1,0:T(8,128)(2,1)} async-done(((bf16[2,64,5504]{2,1,0:T(8,128)(2,1)}), bf16[2,64,5504]{2,1,0:T(8,128)(2,1)}) %all-reduce.2.cloned.1.call-update) | async-done | bytes 1409040 | tf_op jit(solution)/shard_map/psum | solution.py:58
  257.6 1.5 convert_element_type.38
  259.1 12.3 %fusion.1 = bf16[64,2,2048]{2,0,1:T(8,128)(2,1)} fusion(bf16[2,2752,2048]{2,1,0:T(8,128)(2,1)} %param.19, f32[2,64,5504]{2,1,0:T(8,128)S(1)} %convert_element_type.38), kind=kOutput, calls=%fused_computation.5 | convolution fusion | flops 1445216256 | bytes 25952256 | tf_op jit(solution)/shard_map/esf,efd->sed/dot_general | solution.py:63
  271.5 0.4 fusion.6
  271.9 7.3 %psum.23 = f32[128,4]{0,1:T(4,128)S(1)} all-reduce(f32[128,4]{0,1:T(4,128)S(1)} %fusion.6), channel_id=1, replica_groups=mesh['groups'=2,'tok'=4,'mod'=2,'fsdp'=2] {'mod','fsdp'}, use_global_device_ids=true, to_apply=%region_4.5 | all-reduce | flops 512 | bytes 4096 | tf_op jit(solution)/shard_map/psum | solution.py:39
  279.2 0.2 fusion.13
  279.4 15.0 %reduce-scatter.3.cloned.1.call-done = bf16[16,2,2048]{2,0,1:T(8,128)(2,1)} async-done(((bf16[64,2,2048]{2,0,1:T(8,128)(2,1)}), bf16[16,2,2048]{2,0,1:T(8,128)(2,1)}) %reduce-scatter.3.cloned.1.call-update) | async-done | bytes 131088 | tf_op jit(solution)/shard_map/reduce_scatter | solution.py:62
  294.4 2.4 fusion
  296.8 12.9 %reduce-scatter.5.cloned.1.call-done = bf16[128,1024]{1,0:T(8,128)(2,1)} async-done(((bf16[128,2048]{1,0:T(8,128)(2,1)}), bf16[128,1024]{1,0:T(8,128)(2,1)}) %reduce-scatter.5.cloned.1.call-update) | async-done | bytes 262160 | tf_op jit(solution)/shard_map/reduce_scatter | solution.py:75
  (14 shorter events, 0.2 us)
Async XLA Ops:
  6.5 264.9 %copy-start = (bf16[1024,4]{0,1:T(4,128)(2,1)S(1)}, bf16[1024,4]{0,1:T(4,128)(2,1)}, u32[]{:S(2)}) copy-start(bf16[1024,4]{0,1:T(4,128)(2,1)} %param.14) | copy-start | bytes 24580
  6.5 21.8 %all-gather.3.cloned.1.call-start = ((), (), s32[]{:S(2)}) async-start(), calls=%async_computation.2 | async-start | bytes 1310720 | tf_op jit(solution)/shard_map/all_gather | solution.py:22
  7.3 172.4 %all-gather.5.cloned.1.call-start = ((), (), s32[]{:S(2)}) async-start(), calls=%async_computation.3 | async-start | bytes 10485760 | tf_op jit(solution)/shard_map/all_gather | solution.py:26
  8.0 249.5 %all-reduce.2.cloned.1.call-start = ((), (), s32[]{:S(2)}) async-start(), calls=%async_computation.4 | async-start | bytes 2818048 | tf_op jit(solution)/shard_map/psum | solution.py:58
  238.1 56.3 %reduce-scatter.3.cloned.1.call-start = ((), (), s32[]{:S(2)}) async-start(), calls=%async_computation.5 | async-start | bytes 655360 | tf_op jit(solution)/shard_map/reduce_scatter | solution.py:62
  271.4 38.4 %reduce-scatter.5.cloned.1.call-start = ((), (), s32[]{:S(2)}) async-start(), calls=%async_computation.6 | async-start | bytes 786432 | tf_op jit(solution)/shard_map/reduce_scatter | solution.py:75
Sparse Core Ops, SparseCore 0:
  8.9 19.4 all-gather.2
  29.9 149.6 all-gather.4
  238.2 19.2 all-reduce.1
  271.5 22.8 reduce-scatter.2
  296.9 12.7 reduce-scatter.4
where the time goes:
time: 317 us; the launch traced here: 316 us
  waiting for transfers between devices  218 us (69%)
  matrix products  43.1 us (14%)
  blocking collectives  36.4 us (11%)
  between operations  13.8 us (4%)
  other arithmetic  3.74 us (1%)
    all_gather x1, waiting for transfers between devices, local(): lax.all_gather(out_proj, 'tok', axis=0, tiled=True)  151 us
    psum x1, waiting for transfers between devices, local(): lax.psum(partial_in.astype(jnp.bfloat16), 'fsdp').astype(jnp.float32)  19.4 us
    all_gather x1, waiting for transfers between devices, local(): full_context = lax.all_gather(context, ('mod', 'fsdp'), axis=1, tiled=True)  18.3 us
    reduce_scatter x1, waiting for transfers between devices, local(): lax.psum_scatter(jnp.einsum('esf,efd->sed', activation, down_weight, pref...  15 us
    all_gather x1, blocking collectives, local(): piece = lax.all_gather(chosen, 'tok', axis=1, tiled=True)  14.7 us
    reduce_scatter x1, waiting for transfers between devices, local(): lax.psum_scatter(mixed_rows.astype(jnp.bfloat16), 'mod', scatter_dimensio...  12.9 us
    dot_general x1, matrix products, local(): jnp.einsum('esf,efd->sed', activation, down_weight, preferred_element_typ...  12.3 us
    dot_general x1, matrix products, local(): jnp.einsum('esd,edf->esf', piece, gate_weight, preferred_element_type=jnp...  11.3 us
  transfers between devices with their start and end apart: 5, of which 5 were waited for; matrix products, arithmetic and copies ran while one was open for 1% of the time, Pallas kernels for 0%

commit v1 on v0

--- a/solution.py
+++ b/solution.py
@@ -36,8 +36,11 @@
     square_total = lax.psum(squares, ("mod", "fsdp"))
     inverse = lax.rsqrt(square_total / D + 1e-05)
     normed = gained * inverse[:, None]
-    logits = lax.psum(
-        jnp.dot(normed, router_table, precision=lax.Precision.HIGHEST), ("mod", "fsdp")
+    logits = jnp.sum(
+        lax.all_gather(
+            jnp.dot(normed, router_table, precision=lax.Precision.HIGHEST), ("mod", "fsdp")
+        ),
+        axis=0,
     )
     score = jax.nn.sigmoid(logits)
     normed_rows = normed.astype(jnp.bfloat16)

time: 317 us -> 317 us (level)
    psum x1 -> x0, blocking collectives: 7.27 us -> none  [local(): lax.psum(jnp.dot(normed, router_table, precision=lax.Precision.HIGHEST),...]
    all_gather x0 -> x1, blocking collectives: none -> 5.17 us  [local(): lax.all_gather(jnp.dot(normed, router_table, precision=lax.Precision.HIGH...]
where the time goes in v1:
time: 317 us; the launch traced here: 316 us
  waiting for transfers between devices  220 us (69%)
  matrix products  43.1 us (14%)
  blocking collectives  34.3 us (11%)
  between operations  13.8 us (4%)
  other arithmetic  3.76 us (1%)
    all_gather x1, waiting for transfers between devices, local(): lax.all_gather(out_proj, 'tok', axis=0, tiled=True)  151 us
    psum x1, waiting for transfers between devices, local(): lax.psum(partial_in.astype(jnp.bfloat16), 'fsdp').astype(jnp.float32)  19.4 us
    all_gather x1, waiting for transfers between devices, local(): full_context = lax.all_gather(context, ('mod', 'fsdp'), axis=1, tiled=True)  18.3 us
    reduce_scatter x1, waiting for transfers between devices, local(): lax.psum_scatter(jnp.einsum('esf,efd->sed', activation, down_weight, pref...  17.1 us
    all_gather x1, blocking collectives, local(): piece = lax.all_gather(chosen, 'tok', axis=1, tiled=True)  14.7 us
    reduce_scatter x1, waiting for transfers between devices, local(): lax.psum_scatter(mixed_rows.astype(jnp.bfloat16), 'mod', scatter_dimensio...  12.9 us
    dot_general x1, matrix products, local(): jnp.einsum('esf,efd->sed', activation, down_weight, preferred_element_typ...  12.3 us
    dot_general x1, matrix products, local(): jnp.einsum('esd,edf->esf', piece, gate_weight, preferred_element_type=jnp...  11.3 us
  transfers between devices with their start and end apart: 5, of which 5 were waited for; matrix products, arithmetic and copies ran while one was open for 1% of the time, Pallas kernels for 0%

profile of v1, /device:TPU:0, one launch (start us, length us, event | category | flops | bytes accessed | tf_op | source)
XLA Modules:
  0.0 316.3 jit_solution(40605309758779995)
XLA Ops:
  6.5 0.7 all-gather.4.cloned.1.call-update
  7.3 0.7 all-gather.6.cloned.1.call-update
  8.7 0.7 convert_element_type.35
  9.4 0.7 constant_dynamic-slice_fusion.1
  10.1 18.3 %all-gather.4.cloned.1.call-done = bf16[128,4096]{1,0:T(8,128)(2,1)} async-done(((bf16[128,1024]{1,0:T(8,128)(2,1)}), bf16[128,4096]{1,0:T(8,128)(2,1)}) %all-gather.4.cloned.1.call-update) | async-done | bytes 1048592 | tf_op jit(solution)/shard_map/all_gather | solution.py:22
  28.4 151.2 %all-gather.6.cloned.1.call-done = bf16[4096,1024]{1,0:T(8,128)(2,1)} async-done(((bf16[1024,1024]{1,0:T(8,128)(2,1)}), bf16[4096,1024]{1,0:T(8,128)(2,1)}) %all-gather.6.cloned.1.call-update) | async-done | bytes 8388624 | tf_op jit(solution)/shard_map/all_gather | solution.py:26
  179.6 5.0 %multiply_reduce_fusion = (f32[128]{0:T(128)S(1)}, f32[128,1024]{1,0:T(8,128)S(1)}) fusion(bf16[128,4096]{1,0:T(8,128)(2,1)} %all-gather.4.cloned.1.call-done, bf16[4096,1024]{1,0:T(8,128)(2,1)} %all-gather.6.cloned.1.call-done, bf16[128,1024]{1,0:T(8,128)(2,1)} %param.10), kind=kOutput, calls=%fused_computation.13 | convolution fusion | flops 1074265984 | bytes 10224128 | tf_op jit(solution)/shard_map/dot_general | solution.py:24
  184.6 6.8 %psum.14 = f32[128]{0:T(128)S(1)} all-reduce(f32[128]{0:T(128)S(1)} %get-tuple-element.5), channel_id=1, replica_groups=mesh['groups'=2,'tok'=4,'mod'=2,'fsdp'=2] {'mod','fsdp'}, use_global_device_ids=true, to_apply=%region_1.2 | all-reduce | flops 128 | bytes 1024 | tf_op jit(solution)/shard_map/psum | solution.py:36
  191.5 0.1 fusion.7
  191.6 7.6 %all_gather.20 = bf16[128,2048]{1,0:T(8,128)(2,1)S(1)} all-gather(bf16[128,1024]{1,0:T(8,128)(2,1)S(1)} %fusion.7), channel_id=1, replica_groups=mesh['groups'=2,'tok'=4,'mod'=2,'fsdp'=2] {'mod'}, dimensions={1}, use_global_device_ids=true | all-gather | bytes 786432 | tf_op jit(solution)/shard_map/all_gather | solution.py:52
  199.1 0.2 convolution_convert_fusion.3
  199.4 14.7 %all_gather.21 = bf16[2,64,2048]{2,1,0:T(8,128)(2,1)S(1)} all-gather(bf16[2,16,2048]{2,1,0:T(8,128)(2,1)S(1)} %convolution_convert_fusion.3), channel_id=1, replica_groups=mesh['groups'=2,'tok'=4,'mod'=2,'fsdp'=2] {'tok'}, dimensions={1}, use_global_device_ids=true | all-gather | bytes 655360 | tf_op jit(solution)/shard_map/all_gather | solution.py:57
  214.1 11.3 %convolution_convert_fusion = bf16[2,64,2752]{2,1,0:T(8,128)(2,1)S(1)} fusion(bf16[2,64,2048]{2,1,0:T(8,128)(2,1)S(1)} %all_gather.21, bf16[2,2048,2752]{1,2,0:T(8,128)(2,1)} %param.18), kind=kOutput, calls=%fused_computation | convolution fusion | flops 1443192832 | bytes 23773184 | tf_op jit(solution)/shard_map/esd,edf->esf/dot_general | solution.py:59
  225.4 11.3 %convolution_convert_fusion.1 = bf16[2,64,2752]{2,1,0:T(8,128)(2,1)S(1)} fusion(bf16[2,64,2048]{2,1,0:T(8,128)(2,1)S(1)} %all_gather.21, bf16[2,2048,2752]{1,2,0:T(8,128)(2,1)} %param.17), kind=kOutput, calls=%fused_computation.1 | convolution fusion | flops 1443192832 | bytes 23773184 | tf_op jit(solution)/shard_map/esd,edf->esf/dot_general | solution.py:58
  236.7 1.4 pad_maximum_fusion
  238.2 19.4 %all-reduce.2.cloned.1.call-done = bf16[2,64,5504]{2,1,0:T(8,128)(2,1)} async-done(((bf16[2,64,5504]{2,1,0:T(8,128)(2,1)}), bf16[2,64,5504]{2,1,0:T(8,128)(2,1)}) %all-reduce.2.cloned.1.call-update) | async-done | bytes 1409040 | tf_op jit(solution)/shard_map/psum | solution.py:61
  257.6 1.5 convert_element_type.38
  259.1 12.3 %fusion.1 = bf16[64,2,2048]{2,0,1:T(8,128)(2,1)} fusion(bf16[2,2752,2048]{2,1,0:T(8,128)(2,1)} %param.19, f32[2,64,5504]{2,1,0:T(8,128)S(1)} %convert_element_type.38), kind=kOutput, calls=%fused_computation.5 | convolution fusion | flops 1445216256 | bytes 25952256 | tf_op jit(solution)/shard_map/esf,efd->sed/dot_general | solution.py:66
  271.5 0.4 fusion.6
  271.9 5.2 %all-gather = f32[512,4]{0,1:T(4,128)S(1)} all-gather(f32[128,4]{0,1:T(4,128)S(1)} %fusion.6), channel_id=2, replica_groups=mesh['groups'=2,'tok'=4,'mod'=2,'fsdp'=2] {'mod','fsdp'}, dimensions={0}, use_global_device_ids=true | all-gather | bytes 10240 | tf_op jit(solution)/shard_map/all_gather | solution.py:40
  277.1 0.2 fusion.13
  277.3 17.1 %reduce-scatter.3.cloned.1.call-done = bf16[16,2,2048]{2,0,1:T(8,128)(2,1)} async-done(((bf16[64,2,2048]{2,0,1:T(8,128)(2,1)}), bf16[16,2,2048]{2,0,1:T(8,128)(2,1)}) %reduce-scatter.3.cloned.1.call-update) | async-done | bytes 131088 | tf_op jit(solution)/shard_map/reduce_scatter | solution.py:65
  294.4 2.4 fusion
  296.8 12.9 %reduce-scatter.5.cloned.1.call-done = bf16[128,1024]{1,0:T(8,128)(2,1)} async-done(((bf16[128,2048]{1,0:T(8,128)(2,1)}), bf16[128,1024]{1,0:T(8,128)(2,1)}) %reduce-scatter.5.cloned.1.call-update) | async-done | bytes 262160 | tf_op jit(solution)/shard_map/reduce_scatter | solution.py:78
  (16 shorter events, 0.3 us)
Async XLA Ops:
  6.5 264.9 %copy-start = (bf16[1024,4]{0,1:T(4,128)(2,1)S(1)}, bf16[1024,4]{0,1:T(4,128)(2,1)}, u32[]{:S(2)}) copy-start(bf16[1024,4]{0,1:T(4,128)(2,1)} %param.14) | copy-start | bytes 24580
  6.5 21.8 %all-gather.4.cloned.1.call-start = ((), (), s32[]{:S(2)}) async-start(), calls=%async_computation.2 | async-start | bytes 1310720 | tf_op jit(solution)/shard_map/all_gather | solution.py:22
  7.3 172.4 %all-gather.6.cloned.1.call-start = ((), (), s32[]{:S(2)}) async-start(), calls=%async_computation.3 | async-start | bytes 10485760 | tf_op jit(solution)/shard_map/all_gather | solution.py:26
  8.0 249.5 %all-reduce.2.cloned.1.call-start = ((), (), s32[]{:S(2)}) async-start(), calls=%async_computation.4 | async-start | bytes 2818048 | tf_op jit(solution)/shard_map/psum | solution.py:61
  238.1 56.3 %reduce-scatter.3.cloned.1.call-start = ((), (), s32[]{:S(2)}) async-start(), calls=%async_computation.5 | async-start | bytes 655360 | tf_op jit(solution)/shard_map/reduce_scatter | solution.py:65
  271.4 38.4 %reduce-scatter.5.cloned.1.call-start = ((), (), s32[]{:S(2)}) async-start(), calls=%async_computation.6 | async-start | bytes 786432 | tf_op jit(solution)/shard_map/reduce_scatter | solution.py:78
Sparse Core Ops, SparseCore 0:
  8.9 19.4 all-gather.3
  29.9 149.6 all-gather.5
  238.2 19.2 all-reduce.1
  271.5 22.8 reduce-scatter.2
  296.9 12.7 reduce-scatter.4
